TPU v7x, 256 devices: a whole 4x4x8 slice. The times are simulated.
256 devices in a mesh: rows: 256 (over x, y, z, core).
Axes of the slice: x: 4, y: 4, z: 8, core: 2. Of those that a mesh axis runs over, the one named last changes fastest.
Arguments:
- density: float32 [1024, 64, 512], P('rows'), may hold values from -0.75 to 0.75
- send_rows: int32 [256, 13, 2], replicated, may hold values from -1 to 3, as said below
- recv_pos: int32 [1024, 3], replicated, may hold values from 0 to 25, as said below
Outputs:
- purified: float32 [1024, 64, 512], P('rows')
Inputs may be any that keep to these rules, and one draw needn't show every extreme that they name: `send_rows`: entry (d, g, p) is the local block row that device d sends in slot p of its group-g message, to the device at loop position (d - o_g) mod the number of devices; -1 marks an empty slot. Used slots come first, hold distinct rows and number 1 to 2 in a message; some message of every draw uses all 2. `recv_pos`: entry (r, e) = g * 2 + p names a used slot p of the group-g message that the owner of block row r receives; the block row carried there is the column of r's e-th out-of-band block. The 3 entries of a row are distinct.
All inputs are finite; a program needn't handle non-finite values.
Results may differ from a plain program's by a relative error of at most 0.0003.
Values sent between devices are 32-bit elements; how exact they have to be, the bound alone decides.
A program may use at most 64 MiB of HBM per device.

v0:
```python
import jax
import jax.numpy as jnp
from jax import lax
from jax.sharding import PartitionSpec as P

H = 2
CAP = 2


def extended_2(array, sides, width):
    for axis, dim in sides:
        size, length = (lax.axis_size(axis), array.shape[dim])
        up = [(i, (i + 1) % size) for i in range(size)]
        down = [(j, i) for i, j in up]
        last = lax.slice_in_dim(array, length - width, length, axis=dim)
        initial = lax.slice_in_dim(array, 0, width, axis=dim)
        before = lax.ppermute(last, axis, up)
        after = lax.ppermute(initial, axis, down)
        array = jnp.concatenate([before, array, after], axis=dim)
    return array


def shifted(block, axis, distance):
    devices = range(lax.axis_size(axis))
    route = [((i - distance) % len(devices), i) for i in devices]
    return lax.ppermute(block, axis, route)


def offset_list(count_dev):
    levels = count_dev.bit_length() - 1
    forward = [2 ** (position + 1) for position in range(levels - 1)]
    backward = [-(2 ** (position + 1)) for position in range(levels - 2)]
    return forward + backward


def column_table(send_rows, recv_pos, per_dev, count_dev, shifts_by, half_band, slots_cap):
    total_rows = per_dev * count_dev
    offset_values = jnp.array(shifts_by, dtype=jnp.int32)
    global_rows = jnp.arange(total_rows, dtype=jnp.int32)
    owners = global_rows // per_dev
    groups_of = recv_pos // slots_cap
    places = recv_pos % slots_cap
    senders = (owners[:, None] + offset_values[groups_of]) % count_dev
    local_rows = send_rows[senders, groups_of, places]
    far_cols = senders * per_dev + local_rows
    band_cols = (
        global_rows[:, None] + jnp.arange(-half_band, half_band + 1, dtype=jnp.int32)[None, :]
    ) % total_rows
    return jnp.concatenate([band_cols, far_cols], axis=1)


def shards(density, send_rows, recv_pos):
    count_dev = lax.axis_size("rows")
    device = lax.axis_index("rows")
    per_dev = density.shape[0]
    total_rows = per_dev * count_dev
    shifts_by = offset_list(count_dev)
    groups_total = len(shifts_by)
    columns = column_table(send_rows, recv_pos, per_dev, count_dev, shifts_by, H, CAP)
    extended = extended_2(density, (("rows", 0),), H)
    outgoing = [
        density[jnp.maximum(send_rows[device, member], 0)] for member in range(groups_total)
    ]
    arrived = [
        shifted(outgoing[member], "rows", -shifts_by[member] % count_dev)
        for member in range(groups_total)
    ]
    far_stack = jnp.concatenate(arrived, axis=0)
    senders = (device + jnp.array(shifts_by, dtype=jnp.int32)) % count_dev
    far_ids = senders[:, None] * per_dev + jnp.maximum(
        send_rows[senders, jnp.arange(groups_total, dtype=jnp.int32)], 0
    )
    ext_ids = (device * per_dev - H + jnp.arange(per_dev + 2 * H, dtype=jnp.int32)) % total_rows
    avail_ids = jnp.concatenate([ext_ids, far_ids.reshape(-1)])
    avail_cols = columns[avail_ids]
    available = jnp.concatenate([extended, far_stack], axis=0)
    slot_count = columns.shape[1]
    own_cols = lax.dynamic_slice(columns, (device * per_dev, 0), (per_dev, slot_count))
    own_pos = lax.dynamic_slice(recv_pos, (device * per_dev, 0), (per_dev, recv_pos.shape[1]))
    band_index = (
        jnp.arange(per_dev, dtype=jnp.int32)[:, None]
        + jnp.arange(2 * H + 1, dtype=jnp.int32)[None, :]
    )
    local_index = jnp.concatenate([band_index, per_dev + 2 * H + own_pos], axis=1)
    block_width = density.shape[1]

    def gathered_for(row_index):
        picks = local_index[row_index]
        picked = available[picks]
        picked_cols = avail_cols[picks]
        matches = (picked_cols[:, :, None] == own_cols[row_index][None, None, :]).astype(
            jnp.float32
        )
        tiles_view = picked.reshape(slot_count, block_width, slot_count, block_width)
        gathered = jnp.einsum(
            "sut,saub->satb", matches, tiles_view, precision=lax.Precision.HIGHEST
        )
        return gathered.reshape(slot_count * block_width, slot_count * block_width)

    def multiply(left_panel, gathered):
        return jnp.dot(
            left_panel,
            gathered,
            precision=lax.Precision.HIGHEST,
            preferred_element_type=jnp.float32,
        )

    rows_here = jnp.arange(per_dev, dtype=jnp.int32)

    def both_rows(row_index):
        gathered = gathered_for(row_index)
        square_row = multiply(density[row_index], gathered)
        return (square_row, multiply(square_row, gathered))

    square, cube_rows = lax.map(both_rows, rows_here)
    return 3.0 * square - 2.0 * cube_rows


def solution(mesh):
    return jax.shard_map(
        shards,
        mesh=mesh,
        in_specs=(P("rows", None, None), P(), P()),
        out_specs=P("rows", None, None),
        check_vma=False,
    )
```

profile of v0, /device:TPU:57, one launch (start us, length us, event | category | flops | bytes accessed | tf_op | source)
XLA Modules:
  0.0 208.2 jit_solution(13004677111389177327)
XLA Ops:
  0.0 1.2 fusion.59
  1.2 2.3 %gather_fusion.2 = f32[2,64,512]{2,1,0:T(8,128)} fusion(f32[4,64,512]{2,1,0:T(8,128)} %param.7, s32[1024]{0:T(1024)S(1)} %pad_clamp_fusion.14), kind=kCustom, calls=%fused_computation.2 | custom fusion | bytes 524296 | tf_op jit(solution)/shard_map/gather | solution.py:62
  3.5 1.8 fusion.69
  5.4 2.3 %collective-permute-start = (f32[2,64,512]{2,1,0:T(8,128)}, f32[2,64,512]{2,1,0:T(8,128)}, u32[]{:S(2)}, u32[]{:S(2)}) collective-permute-start(f32[2,64,512]{2,1,0:T(8,128)} %get-tuple-element.100), channel_id=1, source_target_pairs={{0,1},{1,2},{2,3},{3,4},{4,5},{5,6},{6,7},{7,8},{8,9},{9,10},{10,1... | collective-permute-start | bytes 786440 | tf_op jit(solution)/shard_map/ppermute | solution.py:17
  7.7 2.3 %gather_fusion.3 = f32[2,64,512]{2,1,0:T(8,128)} fusion(f32[4,64,512]{2,1,0:T(8,128)} %param.7, s32[1024]{0:T(1024)S(1)} %pad_clamp_fusion.13), kind=kCustom, calls=%fused_computation.3 | custom fusion | bytes 524296 | tf_op jit(solution)/shard_map/gather | solution.py:62
  10.0 7.4 %collective-permute-start.3 = (f32[2,64,512]{2,1,0:T(8,128)}, f32[2,64,512]{2,1,0:T(8,128)}, u32[]{:S(2)}, u32[]{:S(2)}) collective-permute-start(f32[2,64,512]{2,1,0:T(8,128)} %gather_fusion.3), channel_id=1, source_target_pairs={{4,0},{5,1},{6,2},{7,3},{8,4},{9,5},{10,6},{11,7},{12,8},{13,9},{1... | collective-permute-start | bytes 786440 | tf_op jit(solution)/shard_map/ppermute | solution.py:26
  17.4 2.3 %gather_fusion.4 = f32[2,64,512]{2,1,0:T(8,128)} fusion(f32[4,64,512]{2,1,0:T(8,128)} %param.7, s32[1024]{0:T(1024)S(1)} %pad_clamp_fusion.12), kind=kCustom, calls=%fused_computation.4 | custom fusion | bytes 524296 | tf_op jit(solution)/shard_map/gather | solution.py:62
  20.0 0.9 copy.36
  20.9 0.8 broadcast_compare_fusion
  22.9 2.5 %copy.44 = s32[256,13,2]{2,0,1:T(8,128)} copy(s32[256,13,2]{0,2,1:T(2,128)} %param.8) | data formatting | bytes 53248 | tf_op args[1]
  28.3 0.6 pad_clamp_fusion.6
  29.5 0.6 pad_clamp_fusion.4
  31.6 1.5 fusion.20
  33.5 29.7 %gather_fusion.15 = s32[3072]{0:T(1024)S(1)} fusion(s32[256,13,2]{0,2,1:T(2,128)S(1)} %copy-done, s32[3072]{0:T(1024)S(1)} %reshape.502), kind=kCustom, calls=%fused_computation.15 | custom fusion | bytes 61440 | tf_op jit(solution)/shard_map/gather | solution.py:44
  63.6 1.9 fusion.15
  65.8 1.4 gather_fusion.16
  67.7 1.7 gather_fusion.5
  69.5 1.7 gather_fusion.6
  71.2 1.7 gather_fusion.7
  73.0 1.7 gather_fusion.8
  74.7 1.7 gather_fusion.9
  76.4 1.7 gather_fusion.10
  78.2 1.7 gather_fusion.11
  79.9 1.7 gather_fusion.12
  81.6 1.7 gather_fusion.13
  83.4 1.7 gather_fusion.14
  86.0 1.0 constant_dynamic-update-slice_fusion.15
  86.9 1.1 constant_dynamic-update-slice_fusion.14
  88.0 8.5 %collective-permute-start.6 = (f32[2,64,512]{2,1,0:T(8,128)S(1)}, f32[2,64,512]{2,1,0:T(8,128)S(1)}, u32[]{:S(2)}, u32[]{:S(2)}) collective-permute-start(f32[2,64,512]{2,1,0:T(8,128)S(1)} %gather_fusion.6), channel_id=1, source_target_pairs={{32,0},{33,1},{34,2},{35,3},{36,4},{37,5},{38,6},{39,7},{40,8},{41... | collective-permute-start | bytes 786440 | tf_op jit(solution)/shard_map/ppermute | solution.py:26
  96.6 1.0 constant_dynamic-update-slice_fusion.13
  97.8 1.0 constant_dynamic-update-slice_fusion.12
  98.9 1.0 constant_dynamic-update-slice_fusion.11
  100.0 1.0 constant_dynamic-update-slice_fusion.10
  101.0 2.2 %collective-permute-start.10 = (f32[2,64,512]{2,1,0:T(8,128)S(1)}, f32[2,64,512]{2,1,0:T(8,128)S(1)}, u32[]{:S(2)}, u32[]{:S(2)}) collective-permute-start(f32[2,64,512]{2,1,0:T(8,128)S(1)} %gather_fusion.10), channel_id=1, source_target_pairs={{252,0},{253,1},{254,2},{255,3},{0,4},{1,5},{2,6},{3,7},{4,8},{5,9... | collective-permute-start | bytes 786440 | tf_op jit(solution)/shard_map/ppermute | solution.py:26
  103.2 4.2 %collective-permute-start.11 = (f32[2,64,512]{2,1,0:T(8,128)S(1)}, f32[2,64,512]{2,1,0:T(8,128)S(1)}, u32[]{:S(2)}, u32[]{:S(2)}) collective-permute-start(f32[2,64,512]{2,1,0:T(8,128)S(1)} %gather_fusion.11), channel_id=1, source_target_pairs={{248,0},{249,1},{250,2},{251,3},{252,4},{253,5},{254,6},{255,7},{0... | collective-permute-start | bytes 786440 | tf_op jit(solution)/shard_map/ppermute | solution.py:26
  107.4 2.9 %collective-permute-start.12 = (f32[2,64,512]{2,1,0:T(8,128)S(1)}, f32[2,64,512]{2,1,0:T(8,128)S(1)}, u32[]{:S(2)}, u32[]{:S(2)}) collective-permute-start(f32[2,64,512]{2,1,0:T(8,128)S(1)} %gather_fusion.12), channel_id=1, source_target_pairs={{240,0},{241,1},{242,2},{243,3},{244,4},{245,5},{246,6},{247,7},{2... | collective-permute-start | bytes 786440 | tf_op jit(solution)/shard_map/ppermute | solution.py:26
  110.3 4.5 %collective-permute-start.13 = (f32[2,64,512]{2,1,0:T(8,128)S(1)}, f32[2,64,512]{2,1,0:T(8,128)S(1)}, u32[]{:S(2)}, u32[]{:S(2)}) collective-permute-start(f32[2,64,512]{2,1,0:T(8,128)S(1)} %gather_fusion.13), channel_id=1, source_target_pairs={{224,0},{225,1},{226,2},{227,3},{228,4},{229,5},{230,6},{231,7},{2... | collective-permute-start | bytes 786440 | tf_op jit(solution)/shard_map/ppermute | solution.py:26
  115.1 0.9 collective-permute-done.11
  116.0 15.5 %collective-permute-done.12 = f32[2,64,512]{2,1,0:T(8,128)S(1)} collective-permute-done((f32[2,64,512]{2,1,0:T(8,128)S(1)}, f32[2,64,512]{2,1,0:T(8,128)S(1)}, u32[]{:S(2)}, u32[]{:S(2)}) %collective-permute-start.12) | collective-permute-done | bytes 262176 | tf_op jit(solution)/shard_map/ppermute | solution.py:26
  131.5 4.9 %collective-permute-done.13 = f32[2,64,512]{2,1,0:T(8,128)S(1)} collective-permute-done((f32[2,64,512]{2,1,0:T(8,128)S(1)}, f32[2,64,512]{2,1,0:T(8,128)S(1)}, u32[]{:S(2)}, u32[]{:S(2)}) %collective-permute-start.13) | collective-permute-done | bytes 262176 | tf_op jit(solution)/shard_map/ppermute | solution.py:26
  136.4 10.3 %collective-permute-done.14 = f32[2,64,512]{2,1,0:T(8,128)S(1)} collective-permute-done((f32[2,64,512]{2,1,0:T(8,128)S(1)}, f32[2,64,512]{2,1,0:T(8,128)S(1)}, u32[]{:S(2)}, u32[]{:S(2)}) %collective-permute-start.14) | collective-permute-done | bytes 262176 | tf_op jit(solution)/shard_map/ppermute | solution.py:26
  146.8 2.0 copy-done.1
  148.8 57.3 %while.12 = (s32[]{:T(128)}, f32[4,64,512]{2,1,0:T(8,128)}, f32[4,64,512]{2,1,0:T(8,128)}, s32[4]{0:T(128)S(1)}, f32[4,64,512]{2,1,0:T(8,128)}, /*index=5*/s32[4...) while((s32[]{:T(128)}, f32[4,64,512]{2,1,0:T(8,128)}, ...), condition=%wide.region_1.2_spmd, body=%wide.region_0.1_spmd.sunk | while | flops 427820576 | bytes 11147439 | solution.py:115
  151.1 2.9 %gather_fusion = f32[8,64,512]{2,1,0:T(8,128)S(1)} fusion(f32[34,64,512]{2,1,0:T(8,128)} %get-tuple-element.192, s32[1024]{0:T(1024)S(1)} %pad_clamp_fusion.16), kind=kCustom, calls=%fused_computation.clone.1 | custom fusion | bytes 2097184 | tf_op jit(solution)/shard_map/while/body/eval_jaxpr/gather | solution.py:89
  155.0 2.4 %convolution_bitcast_fusion.3 = f32[8,64,8,64]{3,2,1,0:T(8,128)} fusion(f32[8,64,8,64]{3,2,1,0:T(8,128)S(1)} %reshape.578, s32[8,8]{1,0:T(8,128)S(1)} %gather_fusion.1, s32[8]{0:T(128)S(1)} %fusion.88), kind=kOutput, calls=%fused_computation.18.clone.1 | convolution fusion | flops 25166336 | bytes 2097440 | tf_op jit(solution)/shard_map/while/body/eval_jaxpr/sut,saub->satb/dot_general | solution.py:95
  157.4 1.9 reshape.579
  159.4 2.3 %bitcast_dynamic-update-slice_fusion.2 = (f32[4,64,512]{2,1,0:T(8,128)}, f32[64,512]{1,0:T(8,128)S(1)}) fusion(f32[4,64,512]{2,1,0:T(8,128)} %get-tuple-element.175, s32[]{:T(128)} %get-tuple-element.174, f32[512,512]{1,0:T(8,128)S(1)} %reshape.579, f32[4,64,512]{2,1,0:T(8,128)} %get-tuple-element.190, s32[]{:T(128)S(6)} %select_n.252), kind=kOutput, calls=%fused_computation.21.clone.1 | convolution fusion | flops 201326592 | bytes 1442308 | tf_op jit(solution)/shard_map/while/body/eval_jaxpr/dot_general | solution.py:101
  161.7 1.4 fusion.89
  165.4 2.9 %gather_fusion = f32[8,64,512]{2,1,0:T(8,128)S(1)} fusion(f32[34,64,512]{2,1,0:T(8,128)} %get-tuple-element.192, s32[1024]{0:T(1024)S(1)} %pad_clamp_fusion.16), kind=kCustom, calls=%fused_computation.clone.1 | custom fusion | bytes 2097184 | tf_op jit(solution)/shard_map/while/body/eval_jaxpr/gather | solution.py:89
  169.3 2.4 %convolution_bitcast_fusion.3 = f32[8,64,8,64]{3,2,1,0:T(8,128)} fusion(f32[8,64,8,64]{3,2,1,0:T(8,128)S(1)} %reshape.578, s32[8,8]{1,0:T(8,128)S(1)} %gather_fusion.1, s32[8]{0:T(128)S(1)} %fusion.88), kind=kOutput, calls=%fused_computation.18.clone.1 | convolution fusion | flops 25166336 | bytes 2097440 | tf_op jit(solution)/shard_map/while/body/eval_jaxpr/sut,saub->satb/dot_general | solution.py:95
  171.8 1.9 reshape.579
  173.7 2.3 %bitcast_dynamic-update-slice_fusion.2 = (f32[4,64,512]{2,1,0:T(8,128)}, f32[64,512]{1,0:T(8,128)S(1)}) fusion(f32[4,64,512]{2,1,0:T(8,128)} %get-tuple-element.175, s32[]{:T(128)} %get-tuple-element.174, f32[512,512]{1,0:T(8,128)S(1)} %reshape.579, f32[4,64,512]{2,1,0:T(8,128)} %get-tuple-element.190, s32[]{:T(128)S(6)} %select_n.252), kind=kOutput, calls=%fused_computation.21.clone.1 | convolution fusion | flops 201326592 | bytes 1442308 | tf_op jit(solution)/shard_map/while/body/eval_jaxpr/dot_general | solution.py:101
  176.0 1.4 fusion.89
  179.8 2.9 %gather_fusion = f32[8,64,512]{2,1,0:T(8,128)S(1)} fusion(f32[34,64,512]{2,1,0:T(8,128)} %get-tuple-element.192, s32[1024]{0:T(1024)S(1)} %pad_clamp_fusion.16), kind=kCustom, calls=%fused_computation.clone.1 | custom fusion | bytes 2097184 | tf_op jit(solution)/shard_map/while/body/eval_jaxpr/gather | solution.py:89
  183.7 2.4 %convolution_bitcast_fusion.3 = f32[8,64,8,64]{3,2,1,0:T(8,128)} fusion(f32[8,64,8,64]{3,2,1,0:T(8,128)S(1)} %reshape.578, s32[8,8]{1,0:T(8,128)S(1)} %gather_fusion.1, s32[8]{0:T(128)S(1)} %fusion.88), kind=kOutput, calls=%fused_computation.18.clone.1 | convolution fusion | flops 25166336 | bytes 2097440 | tf_op jit(solution)/shard_map/while/body/eval_jaxpr/sut,saub->satb/dot_general | solution.py:95
  186.1 1.9 reshape.579
  188.0 2.3 %bitcast_dynamic-update-slice_fusion.2 = (f32[4,64,512]{2,1,0:T(8,128)}, f32[64,512]{1,0:T(8,128)S(1)}) fusion(f32[4,64,512]{2,1,0:T(8,128)} %get-tuple-element.175, s32[]{:T(128)} %get-tuple-element.174, f32[512,512]{1,0:T(8,128)S(1)} %reshape.579, f32[4,64,512]{2,1,0:T(8,128)} %get-tuple-element.190, s32[]{:T(128)S(6)} %select_n.252), kind=kOutput, calls=%fused_computation.21.clone.1 | convolution fusion | flops 201326592 | bytes 1442308 | tf_op jit(solution)/shard_map/while/body/eval_jaxpr/dot_general | solution.py:101
  190.4 1.4 fusion.89
  194.1 2.9 %gather_fusion = f32[8,64,512]{2,1,0:T(8,128)S(1)} fusion(f32[34,64,512]{2,1,0:T(8,128)} %get-tuple-element.192, s32[1024]{0:T(1024)S(1)} %pad_clamp_fusion.16), kind=kCustom, calls=%fused_computation.clone.1 | custom fusion | bytes 2097184 | tf_op jit(solution)/shard_map/while/body/eval_jaxpr/gather | solution.py:89
  198.0 2.4 %convolution_bitcast_fusion.3 = f32[8,64,8,64]{3,2,1,0:T(8,128)} fusion(f32[8,64,8,64]{3,2,1,0:T(8,128)S(1)} %reshape.578, s32[8,8]{1,0:T(8,128)S(1)} %gather_fusion.1, s32[8]{0:T(128)S(1)} %fusion.88), kind=kOutput, calls=%fused_computation.18.clone.1 | convolution fusion | flops 25166336 | bytes 2097440 | tf_op jit(solution)/shard_map/while/body/eval_jaxpr/sut,saub->satb/dot_general | solution.py:95
  200.4 1.9 reshape.579
  202.4 2.3 %bitcast_dynamic-update-slice_fusion.2 = (f32[4,64,512]{2,1,0:T(8,128)}, f32[64,512]{1,0:T(8,128)S(1)}) fusion(f32[4,64,512]{2,1,0:T(8,128)} %get-tuple-element.175, s32[]{:T(128)} %get-tuple-element.174, f32[512,512]{1,0:T(8,128)S(1)} %reshape.579, f32[4,64,512]{2,1,0:T(8,128)} %get-tuple-element.190, s32[]{:T(128)S(6)} %select_n.252), kind=kOutput, calls=%fused_computation.21.clone.1 | convolution fusion | flops 201326592 | bytes 1442308 | tf_op jit(solution)/shard_map/while/body/eval_jaxpr/dot_general | solution.py:101
  204.7 1.4 fusion.89
  206.1 2.1 %multiply_subtract_fusion = f32[4,64,512]{2,1,0:T(8,128)} fusion(f32[4,64,512]{2,1,0:T(8,128)} %get-tuple-element.54, f32[4,64,512]{2,1,0:T(8,128)} %get-tuple-element.53), kind=kLoop, calls=%fused_computation.68 | loop fusion | flops 393216 | bytes 1572864 | tf_op jit(solution)/shard_map/sub | solution.py:116
  (104 shorter events, 15.9 us)
Async XLA Ops:
  0.0 33.4 %copy-start = (s32[256,13,2]{0,2,1:T(2,128)S(1)}, s32[256,13,2]{0,2,1:T(2,128)}, u32[]{:S(2)}) copy-start(s32[256,13,2]{0,2,1:T(2,128)} %param.8) | copy-start | bytes 79876
  3.5 94.0 %collective-permute-start.2 = (f32[2,64,512]{2,1,0:T(8,128)}, f32[2,64,512]{2,1,0:T(8,128)}, u32[]{:S(2)}, u32[]{:S(2)}) collective-permute-start(f32[2,64,512]{2,1,0:T(8,128)} %gather_fusion.2), channel_id=1, source_target_pairs={{2,0},{3,1},{4,2},{5,3},{6,4},{7,5},{8,6},{9,7},{10,8},{11,9},{12,... | collective-permute-start | bytes 786440 | tf_op jit(solution)/shard_map/ppermute | solution.py:26
  5.4 80.3 %collective-permute-start = (f32[2,64,512]{2,1,0:T(8,128)}, f32[2,64,512]{2,1,0:T(8,128)}, u32[]{:S(2)}, u32[]{:S(2)}) collective-permute-start(f32[2,64,512]{2,1,0:T(8,128)} %get-tuple-element.100), channel_id=1, source_target_pairs={{0,1},{1,2},{2,3},{3,4},{4,5},{5,6},{6,7},{7,8},{8,9},{9,10},{10,1... | collective-permute-start | bytes 786440 | tf_op jit(solution)/shard_map/ppermute | solution.py:17
  7.7 80.3 %collective-permute-start.1 = (f32[2,64,512]{2,1,0:T(8,128)}, f32[2,64,512]{2,1,0:T(8,128)}, u32[]{:S(2)}, u32[]{:S(2)}) collective-permute-start(f32[2,64,512]{2,1,0:T(8,128)} %get-tuple-element.99), channel_id=1, source_target_pairs={{1,0},{2,1},{3,2},{4,3},{5,4},{6,5},{7,6},{8,7},{9,8},{10,9},{11,1... | collective-permute-start | bytes 786440 | tf_op jit(solution)/shard_map/ppermute | solution.py:18
  10.0 88.8 %collective-permute-start.3 = (f32[2,64,512]{2,1,0:T(8,128)}, f32[2,64,512]{2,1,0:T(8,128)}, u32[]{:S(2)}, u32[]{:S(2)}) collective-permute-start(f32[2,64,512]{2,1,0:T(8,128)} %gather_fusion.3), channel_id=1, source_target_pairs={{4,0},{5,1},{6,2},{7,3},{8,4},{9,5},{10,6},{11,7},{12,8},{13,9},{1... | collective-permute-start | bytes 786440 | tf_op jit(solution)/shard_map/ppermute | solution.py:26
  19.7 80.1 %collective-permute-start.4 = (f32[2,64,512]{2,1,0:T(8,128)}, f32[2,64,512]{2,1,0:T(8,128)}, u32[]{:S(2)}, u32[]{:S(2)}) collective-permute-start(f32[2,64,512]{2,1,0:T(8,128)} %gather_fusion.4), channel_id=1, source_target_pairs={{8,0},{9,1},{10,2},{11,3},{12,4},{13,5},{14,6},{15,7},{16,8},{17,9... | collective-permute-start | bytes 786440 | tf_op jit(solution)/shard_map/ppermute | solution.py:26
  20.9 10.6 %copy-start.2 = (s32[1024,3]{1,0:T(8,128)}, s32[1024,3]{1,0:T(8,128)S(1)}, u32[]{:S(2)}) copy-start(s32[1024,3]{1,0:T(8,128)S(1)} %copy.36) | copy-start | bytes 36868
  21.7 9.9 %copy-start.5 = (s32[1024]{0:T(1024)}, s32[1024]{0:T(1024)S(1)}, u32[]{:S(2)}) copy-start(s32[1024]{0:T(1024)S(1)} %add_select_fusion.5) | copy-start | bytes 12292
  31.6 1.8 copy-start.4
  33.4 30.1 %copy-start.3 = (s32[1024,3]{1,0:T(8,128)S(1)}, s32[1024,3]{1,0:T(8,128)}, u32[]{:S(2)}) copy-start(s32[1024,3]{1,0:T(8,128)} %copy-done.2) | copy-start | bytes 36868
  33.4 30.1 %copy-start.6 = (s32[1024]{0:T(1024)S(1)}, s32[1024]{0:T(1024)}, u32[]{:S(2)}) copy-start(s32[1024]{0:T(1024)} %copy-done.5) | copy-start | bytes 12292
  33.4 32.1 %copy-start.8 = (s32[5]{0:T(128)S(1)}, s32[5]{0:T(128)}, u32[]{:S(2)}) copy-start(s32[5]{0:T(128)} %iota_add_fusion.1) | copy-start | bytes 64
  33.4 32.3 %copy-start.9 = (s32[13]{0:T(128)S(1)}, s32[13]{0:T(128)}, u32[]{:S(2)}) copy-start(s32[13]{0:T(128)} %constant.162.clone) | copy-start | bytes 160
  63.2 4.5 %copy-start.7 = (s32[4,5]{1,0:T(4,128)S(1)}, s32[4,5]{1,0:T(4,128)}, u32[]{:S(2)}) copy-start(s32[4,5]{1,0:T(4,128)} %iota_add_fusion) | copy-start | bytes 244
  85.7 15.3 %collective-permute-start.5 = (f32[2,64,512]{2,1,0:T(8,128)S(1)}, f32[2,64,512]{2,1,0:T(8,128)S(1)}, u32[]{:S(2)}, u32[]{:S(2)}) collective-permute-start(f32[2,64,512]{2,1,0:T(8,128)S(1)} %gather_fusion.5), channel_id=1, source_target_pairs={{16,0},{17,1},{18,2},{19,3},{20,4},{21,5},{22,6},{23,7},{24,8},{25... | collective-permute-start | bytes 786440 | tf_op jit(solution)/shard_map/ppermute | solution.py:26
  88.0 15.2 %collective-permute-start.6 = (f32[2,64,512]{2,1,0:T(8,128)S(1)}, f32[2,64,512]{2,1,0:T(8,128)S(1)}, u32[]{:S(2)}, u32[]{:S(2)}) collective-permute-start(f32[2,64,512]{2,1,0:T(8,128)S(1)} %gather_fusion.6), channel_id=1, source_target_pairs={{32,0},{33,1},{34,2},{35,3},{36,4},{37,5},{38,6},{39,7},{40,8},{41... | collective-permute-start | bytes 786440 | tf_op jit(solution)/shard_map/ppermute | solution.py:26
  97.5 9.9 %collective-permute-start.7 = (f32[2,64,512]{2,1,0:T(8,128)S(1)}, f32[2,64,512]{2,1,0:T(8,128)S(1)}, u32[]{:S(2)}, u32[]{:S(2)}) collective-permute-start(f32[2,64,512]{2,1,0:T(8,128)S(1)} %gather_fusion.7), channel_id=1, source_target_pairs={{64,0},{65,1},{66,2},{67,3},{68,4},{69,5},{70,6},{71,7},{72,8},{73... | collective-permute-start | bytes 786440 | tf_op jit(solution)/shard_map/ppermute | solution.py:26
  98.8 11.5 %collective-permute-start.8 = (f32[2,64,512]{2,1,0:T(8,128)S(1)}, f32[2,64,512]{2,1,0:T(8,128)S(1)}, u32[]{:S(2)}, u32[]{:S(2)}) collective-permute-start(f32[2,64,512]{2,1,0:T(8,128)S(1)} %gather_fusion.8), channel_id=1, source_target_pairs={{128,0},{129,1},{130,2},{131,3},{132,4},{133,5},{134,6},{135,7},{1... | collective-permute-start | bytes 786440 | tf_op jit(solution)/shard_map/ppermute | solution.py:26
  99.9 15.0 %collective-permute-start.9 = (f32[2,64,512]{2,1,0:T(8,128)S(1)}, f32[2,64,512]{2,1,0:T(8,128)S(1)}, u32[]{:S(2)}, u32[]{:S(2)}) collective-permute-start(f32[2,64,512]{2,1,0:T(8,128)S(1)} %gather_fusion.9), channel_id=1, source_target_pairs={{254,0},{255,1},{0,2},{1,3},{2,4},{3,5},{4,6},{5,7},{6,8},{7,9},{8... | collective-permute-start | bytes 786440 | tf_op jit(solution)/shard_map/ppermute | solution.py:26
  101.0 14.1 %collective-permute-start.10 = (f32[2,64,512]{2,1,0:T(8,128)S(1)}, f32[2,64,512]{2,1,0:T(8,128)S(1)}, u32[]{:S(2)}, u32[]{:S(2)}) collective-permute-start(f32[2,64,512]{2,1,0:T(8,128)S(1)} %gather_fusion.10), channel_id=1, source_target_pairs={{252,0},{253,1},{254,2},{255,3},{0,4},{1,5},{2,6},{3,7},{4,8},{5,9... | collective-permute-start | bytes 786440 | tf_op jit(solution)/shard_map/ppermute | solution.py:26
  103.2 12.8 %collective-permute-start.11 = (f32[2,64,512]{2,1,0:T(8,128)S(1)}, f32[2,64,512]{2,1,0:T(8,128)S(1)}, u32[]{:S(2)}, u32[]{:S(2)}) collective-permute-start(f32[2,64,512]{2,1,0:T(8,128)S(1)} %gather_fusion.11), channel_id=1, source_target_pairs={{248,0},{249,1},{250,2},{251,3},{252,4},{253,5},{254,6},{255,7},{0... | collective-permute-start | bytes 786440 | tf_op jit(solution)/shard_map/ppermute | solution.py:26
  107.4 24.1 %collective-permute-start.12 = (f32[2,64,512]{2,1,0:T(8,128)S(1)}, f32[2,64,512]{2,1,0:T(8,128)S(1)}, u32[]{:S(2)}, u32[]{:S(2)}) collective-permute-start(f32[2,64,512]{2,1,0:T(8,128)S(1)} %gather_fusion.12), channel_id=1, source_target_pairs={{240,0},{241,1},{242,2},{243,3},{244,4},{245,5},{246,6},{247,7},{2... | collective-permute-start | bytes 786440 | tf_op jit(solution)/shard_map/ppermute | solution.py:26
  110.3 26.1 %collective-permute-start.13 = (f32[2,64,512]{2,1,0:T(8,128)S(1)}, f32[2,64,512]{2,1,0:T(8,128)S(1)}, u32[]{:S(2)}, u32[]{:S(2)}) collective-permute-start(f32[2,64,512]{2,1,0:T(8,128)S(1)} %gather_fusion.13), channel_id=1, source_target_pairs={{224,0},{225,1},{226,2},{227,3},{228,4},{229,5},{230,6},{231,7},{2... | collective-permute-start | bytes 786440 | tf_op jit(solution)/shard_map/ppermute | solution.py:26
  114.9 31.8 %collective-permute-start.14 = (f32[2,64,512]{2,1,0:T(8,128)S(1)}, f32[2,64,512]{2,1,0:T(8,128)S(1)}, u32[]{:S(2)}, u32[]{:S(2)}) collective-permute-start(f32[2,64,512]{2,1,0:T(8,128)S(1)} %gather_fusion.14), channel_id=1, source_target_pairs={{192,0},{193,1},{194,2},{195,3},{196,4},{197,5},{198,6},{199,7},{2... | collective-permute-start | bytes 786440 | tf_op jit(solution)/shard_map/ppermute | solution.py:26
  146.7 2.0 copy-start.1
where the time goes:
time: 210 us; the launch traced here: 208 us
  local copies, waits for them, and re-layouts  95.8 us (46%)
  starting transfers between devices  33.1 us (16%)
  waiting for transfers between devices  31.6 us (15%)
  matrix products  24.6 us (12%)
  other arithmetic  15.4 us (7%)
  loops' own time  7.1 us (3%)
    ppermute x13, waiting for transfers between devices, shifted(): return lax.ppermute(block, axis, route)  31.6 us
    ppermute x13, starting transfers between devices, shifted(): return lax.ppermute(block, axis, route)  30.8 us
    gather x2, local copies, waits for them, and re-layouts, column_table(): local_rows = send_rows[senders, groups_of, places]  30.1 us
    gather x13, local copies, waits for them, and re-layouts, shards(): density[jnp.maximum(send_rows[device, member], 0)]  24.2 us
    dot_general x8, matrix products, multiply(): jnp.dot(left_panel, gathered, precision=lax.Precision.HIGHEST, preferred_...  14.9 us
    unnamed x37, local copies, waits for them, and re-layouts  11.6 us
    gather x4, local copies, waits for them, and re-layouts, gathered_for(): picked = available[picks]  11.5 us
    dot_general x4, matrix products, gathered_for(): jnp.einsum('sut,saub->satb', matches, tiles_view, precision=lax.Precision...  9.74 us
  transfers between devices with their start and end apart: 15, of which 4 were waited for; matrix products, arithmetic and copies ran while one was open for 37% of the time, Pallas kernels for 0%

commit v1 on v0

v1 whole, which is shorter than its diff:
```python
import functools

import jax
import jax.numpy as jnp
from jax import lax
from jax.experimental import pallas as pl
from jax.experimental.pallas import tpu as pltpu
from jax.sharding import PartitionSpec as P

MESH = pl.DeviceIdType.MESH
B = 64
ORDER = (2, 9, 1, 8, 0, 7, 3, 10, 4, 11, 5, 12, 6)
PANELS = 5


def offset_list(count_dev):
    levels = count_dev.bit_length() - 1
    forward = [2 ** (position + 1) for position in range(levels - 1)]
    backward = [-(2 ** (position + 1)) for position in range(levels - 2)]
    return forward + backward


def flag(condition):
    return jnp.where(condition, 1.0, 0.0).astype(jnp.float32)


def kernel(
    n, offs, x_hbm, sr, rp, out,
    own, left, right, pack, recv, gh, gl, sband, table,
    own_sem, send_sem, recv_sem, halo_send, halo_recv,
):
    me = lax.axis_index("rows")
    rows = n * 4

    def device(step):
        return {"rows": lax.rem(me + step + n, n)}

    barrier = pltpu.get_barrier_semaphore()
    partners = sorted(set(offs) | set(-o for o in offs if o * 2 != n) | {1, -1})
    for step in partners:
        pl.semaphore_signal(barrier, inc=1, device_id=device(step), device_id_type=MESH)

    loads = [
        pltpu.make_async_copy(x_hbm.at[:, :, pl.ds(128 * j, 128)], own.at[j], own_sem.at[j])
        for j in range(4)
    ]
    for load in loads:
        load.start()
    for index, value in enumerate(offs):
        table[index] = value
    lane = lax.broadcasted_iota(jnp.int32, (B, 128), 1)
    low = lane < B
    for load in loads:
        load.wait()

    def tile(k, j):
        if k < 2:
            return left[j, k]
        return right[j, k - 6] if k > 5 else own[j, k - 2]

    def turn(panel):
        return pltpu.roll(panel, B, 1)

    def pack_group(g, carry):
        first = jnp.maximum(sr[g, 0, me], 0)
        second = jnp.maximum(sr[g, 1, me], 0)
        for slot, row in enumerate((first, second)):
            pack[g, 2 * slot] = jnp.where(low, own[1, row], own[2, row])
            pack[g, 2 * slot + 1] = own[3, row]
        delta = jnp.clip(second - first, -2, 2)
        one = own[jnp.where(delta >= 2, 2, jnp.where(delta == 1, 1, 0)), first]
        two = own[jnp.where(delta <= -2, 2, jnp.where(delta == -1, 1, 0)), second]
        odd = flag(jnp.abs(delta) == 1)
        even = 1.0 - odd
        pack[g, 4] = jnp.where(low, odd * turn(one) + even * one, odd * two + even * turn(two))
        return carry

    lax.fori_loop(0, len(offs), pack_group, 0)
    pl.semaphore_wait(barrier, len(partners))

    copies = []
    for g in ORDER:
        copies.append(pltpu.make_async_remote_copy(
            src_ref=pack.at[g], dst_ref=recv.at[pl.ds(g * PANELS, PANELS)],
            send_sem=send_sem.at[g], recv_sem=recv_sem.at[g],
            device_id=device(-offs[g]), device_id_type=MESH,
        ))
    pieces = (
        (1, own.at[pl.ds(1, 2), pl.ds(2, 2)], left.at[pl.ds(1, 2)]),
        (1, own.at[0, 3], left.at[0, 1]),
        (-1, own.at[pl.ds(0, 2), pl.ds(0, 2)], right),
    )
    halo = [
        pltpu.make_async_remote_copy(
            src_ref=source, dst_ref=target, send_sem=halo_send.at[index], recv_sem=halo_recv.at[index],
            device_id=device(step), device_id_type=MESH,
        )
        for index, (step, source, target) in enumerate(pieces)
    ]
    for copy in halo + copies:
        copy.start()

    def far_id(row, e):
        where = rp[e, row]
        group = lax.div(where, 2)
        sender = (lax.div(row, 4) + table[group] + n) % n
        return sender * 4 + jnp.maximum(sr[group, where - 2 * group, sender], 0)

    def split(value):
        high = value.astype(jnp.bfloat16)
        return high, (value - high.astype(jnp.float32)).astype(jnp.bfloat16)

    def put(i, s, j, value):
        high, rest = split(value)
        gh[i, pl.ds(s * B, B), pl.ds(j * 128, 128)] = high
        gl[i, pl.ds(s * B, B), pl.ds(j * 128, 128)] = rest

    def product(left, right_high, right_rest):
        high, rest = split(left)
        both = jnp.concatenate([high, rest], axis=0)
        wide = jnp.dot(both, right_high, preferred_element_type=jnp.float32)
        return wide[:B] + wide[B:] + jnp.dot(high, right_rest, preferred_element_type=jnp.float32)

    zero = jnp.zeros((B, 128), jnp.float32)

    def halves(first, second):
        return jnp.where(low, first, second)

    for copy in halo:
        copy.wait()

    def narrow(i, first):
        return jnp.concatenate([own[first, i], own[first + 1, i]], axis=1)

    ids = [[far_id(me * 4 + i, e) for e in range(3)] for i in range(4)]
    for i in range(4):
        for s in range(5):
            k = i + s
            if s == 2:
                for j in range(4):
                    put(i, s, j, own[j, i])
                continue
            fourth = zero
            if s == 0:
                put(i, s, 0, tile(k, 1))
                put(i, s, 1, halves(tile(k, 2), zero))
            elif s == 1:
                r0, r1, r2 = turn(tile(k, 0)), turn(tile(k, 1)), turn(tile(k, 2))
                put(i, s, 0, halves(r0, r1))
                put(i, s, 1, halves(r1, r2))
            elif s == 3:
                r0, r1 = turn(tile(k, 0)), turn(tile(k, 1))
                put(i, s, 0, halves(zero, r0))
                put(i, s, 1, halves(r0, r1))
                fourth = r1
            else:
                put(i, s, 0, zero)
                put(i, s, 1, tile(k, 0))
                fourth = tile(k, 1)
            if k < 2 or k > 5:
                put(i, s, 2, halves(fourth, zero))
                put(i, s, 3, zero)
                continue
            meet = [[flag(ids[i][e] == ids[k - 2][f]) for f in range(3)] for e in range(3)]
            f2, f3 = tile(k, 2), tile(k, 3)
            g2, g3 = turn(f2), turn(f3)
            put(i, s, 2, halves(fourth, meet[0][0] * f2 + meet[0][1] * g3 + meet[0][2] * f3))
            put(i, s, 3, halves(
                meet[1][0] * g2 + meet[1][1] * f3 + meet[1][2] * g3,
                meet[2][0] * f2 + meet[2][1] * g3 + meet[2][2] * f3,
            ))
        sband[i] = product(narrow(i, 0), gh[i, pl.ds(0, 256), :], gl[i, pl.ds(0, 256), :])

    for copy in copies:
        copy.wait()

    def far_row(i, carry):
        row = me * 4 + i
        mine = [far_id(row, e) for e in range(3)]
        slots = [rp[e, row] for e in range(3)]
        groups = [lax.div(slot, 2) for slot in slots]
        columns = [(row - 2 + t + rows) % rows for t in range(5)] + mine
        for e in range(3):
            place = slots[e] - 2 * groups[e]
            theirs = [far_id(mine[e], f) for f in range(3)]
            start = groups[e] * PANELS
            a, b, c = recv[start + 2 * place], recv[start + 2 * place + 1], recv[start + 4]
            ra, rb, rc = turn(a), turn(b), turn(c)
            for j in range(4):
                parts = []
                for half in range(2):
                    t = 2 * j + half
                    far = [flag(column == columns[t]) for column in theirs]
                    weight = [0.0, far[0], far[1], far[2], 0.0, 0.0]
                    if half == 1:
                        weight = [far[0], 0.0, far[2], far[1], 0.0, 0.0]
                    if t >= 5:
                        if t - 5 == e:
                            weight[half] = 1.0
                        else:
                            distance = jnp.abs(mine[t - 5] - mine[e])
                            cross = jnp.logical_and(groups[t - 5] == groups[e], distance <= 2)
                            weight[4] = flag(jnp.logical_and(cross, place == half))
                            weight[5] = flag(jnp.logical_and(cross, place != half))
                    parts.append(weight)
                value = zero
                for source, left, right in zip((a, ra, b, rb, c, rc), parts[0], parts[1]):
                    if isinstance(left, float) and isinstance(right, float) and left == right == 0.0:
                        continue
                    value = value + halves(jnp.full((B, 128), left), jnp.full((B, 128), right)) * source
                put(i, 5 + e, j, value)
        square = sband[i] + product(
            narrow(i, 2), gh[i, pl.ds(256, 256), :], gl[i, pl.ds(256, 256), :]
        )
        out[i] = 3.0 * square - 2.0 * product(square, gh[i], gl[i])
        return carry

    lax.fori_loop(0, 4, far_row, 0)


def shards(density, send_rows, recv_pos):
    n = lax.axis_size("rows")
    offs = offset_list(n)
    groups = len(offs)
    dma = pltpu.SemaphoreType.DMA
    return pl.pallas_call(
        functools.partial(kernel, n, offs),
        out_shape=jax.ShapeDtypeStruct(density.shape, jnp.float32),
        in_specs=[
            pl.BlockSpec(memory_space=pl.ANY),
            pl.BlockSpec(memory_space=pltpu.SMEM),
            pl.BlockSpec(memory_space=pltpu.SMEM),
        ],
        out_specs=pl.BlockSpec(memory_space=pltpu.VMEM),
        scratch_shapes=[
            pltpu.VMEM((4, 4, B, 128), jnp.float32),
            pltpu.VMEM((3, 2, B, 128), jnp.float32),
            pltpu.VMEM((2, 2, B, 128), jnp.float32),
            pltpu.VMEM((groups, PANELS, B, 128), jnp.float32),
            pltpu.VMEM((groups * PANELS, B, 128), jnp.float32),
            pltpu.VMEM((4, 512, 512), jnp.bfloat16),
            pltpu.VMEM((4, 512, 512), jnp.bfloat16),
            pltpu.VMEM((4, B, 512), jnp.float32),
            pltpu.SMEM((16,), jnp.int32),
            dma((4,)), dma((groups,)), dma((groups,)), dma((3,)), dma((3,)),
        ],
        compiler_params=pltpu.CompilerParams(collective_id=0, has_side_effects=True),
    )(density, jnp.transpose(send_rows, (1, 2, 0)), jnp.transpose(recv_pos, (1, 0)))


def solution(mesh):
    return jax.shard_map(
        shards,
        mesh=mesh,
        in_specs=(P("rows", None, None), P(), P()),
        out_specs=P("rows", None, None),
        check_vma=False,
    )
```

time: 210 us -> 48.6 us (0.23)
  the two profiles are of different devices: /device:TPU:57 before, /device:TPU:1 now
where the time goes in v1:
time: 48.6 us; the launch traced here: 48.3 us
  Pallas kernels  46.4 us (95%)
  local copies, waits for them, and re-layouts  1.87 us (4%)
    pallas_call x1, Pallas kernels, shards(): pl.pallas_call(functools.partial(kernel, n, offs), out_shape=jax.ShapeDty...  46.4 us
    unnamed x1, local copies, waits for them, and re-layouts  1.87 us

profile of v1, /device:TPU:1, one launch (start us, length us, event | category | flops | bytes accessed | tf_op | source)
XLA Modules:
  0.0 48.3 jit_solution(12198035302566781219)
XLA Ops:
  0.0 46.4 %shard_map.37 = f32[4,64,512]{2,1,0:T(8,128)} custom-call(f32[4,64,512]{2,1,0:T(8,128)} %x_hbm.1, s32[13,2,256]{2,1,0:T(2,128)} %bitcast.2, s32[3,1024]{1,0:T(4,128)} %bitcast.3), custom_call_target="tpu_custom_call" | custom-call | tf_op jit(solution)/shard_map/pallas_call | solution.py:226
  46.5 1.9 %copy.5 = f32[4,64,512]{2,1,0:T(8,128)} copy(f32[4,64,512]{2,1,0:T(8,128)} %shard_map.37) | data formatting | bytes 1048576
